TPU v7x, 32 devices: a whole 2x2x4 slice. The times are simulated.
32 devices in a mesh: gx: 4 (over z), gy: 8 (over y, x, core).
Axes of the slice: x: 2, y: 2, z: 4, core: 2. Of those that a mesh axis runs over, the one named last changes fastest.
Arguments:
- right_side: float32 [2048, 4096], P('gx', 'gy'), may hold values from -8 to 8
- drift_x: float32 [2048, 4096], P('gx', 'gy'), may hold values from -0.9 to 0.9
- drift_y: float32 [2048, 4096], P('gx', 'gy'), may hold values from -0.9 to 0.9
- sketch_rows: float32 [256, 2048], P(None, 'gx'), may hold values from -0.375 to 0.375
- sketch_cols: float32 [256, 4096], P(None, 'gy'), may hold values from -6 to 6
Outputs:
- solution: float32 [2048, 4096], P('gx', 'gy')
- residual: float32 [2048, 4096], P('gx', 'gy')
All inputs are finite; a program needn't handle non-finite values.
Results may differ from a plain program's by a relative error of at most 0.0003.
Values sent between devices are 32-bit elements; how exact they have to be, the bound alone decides.
A program may use at most 64 MiB of HBM per device.

v0:
```python
import jax
import jax.numpy as jnp
from jax import lax
from jax.sharding import PartitionSpec as P

ITERS = 4
shift_value = 0.05


def padded_2(cells, sides, width):
    for axis, dim in sides:
        count = lax.axis_size(axis)
        ends = count - 1
        head = lax.slice_in_dim(cells, 0, width, axis=dim)
        tail = lax.slice_in_dim(cells, cells.shape[dim] - width, cells.shape[dim], axis=dim)
        cells = jnp.concatenate(
            [
                lax.ppermute(tail, axis, [(i, (i + 1) % count) for i in range(ends)]),
                cells,
                lax.ppermute(head, axis, [((i + 1) % count, i) for i in range(ends)]),
            ],
            axis=dim,
        )
    return cells


def stencil(padded, field, drift_x, drift_y):
    upper_cells = padded[:-2, 1:-1]
    lower_cells = padded[2:, 1:-1]
    left_cells = padded[1:-1, :-2]
    right_cells = padded[1:-1, 2:]
    return (
        (4.0 + shift_value) * field
        - (1.0 + drift_x) * upper_cells
        - (1.0 - drift_x) * lower_cells
        - (1.0 + drift_y) * left_cells
        - (1.0 - drift_y) * right_cells
    )


def solve_small(hessenberg, beta_norm):
    gram_matrix = jnp.dot(hessenberg.T, hessenberg, precision=lax.Precision.HIGHEST)
    target = beta_norm * hessenberg[0]
    factor = jnp.linalg.cholesky(gram_matrix)
    count = hessenberg.shape[1]
    forward = []
    for row in range(count):
        acc = target[row]
        for col in range(row):
            acc = acc - factor[row, col] * forward[col]
        forward.append(acc / factor[row, row])
    backward = [None] * count
    for row in reversed(range(count)):
        acc = forward[row]
        for col in range(row + 1, count):
            acc = acc - factor[col, row] * backward[col]
        backward[row] = acc / factor[row, row]
    return backward


def body(right_side, drift_x, drift_y, sketch_rows, sketch_cols):

    def sketch(field):
        product = jnp.dot(field, sketch_cols.T, precision=lax.Precision.HIGHEST)
        partial_value = jnp.einsum(
            "ki,ik->k", sketch_rows, product, precision=lax.Precision.HIGHEST
        )
        return lax.psum(partial_value, ("gx", "gy"))

    first_sketch = sketch(right_side)
    beta_norm = jnp.sqrt(jnp.sum(first_sketch * first_sketch))
    basis_vectors = [right_side / beta_norm]
    sketched = [first_sketch / beta_norm]
    images = []
    columns = []
    for column in range(ITERS):
        current = basis_vectors[column]
        padded = padded_2(current, (("gx", 0), ("gy", 1)), 1)
        applied = stencil(padded, current, drift_x, drift_y)
        images.append(applied)
        sketch_image = sketch(applied)
        sketch_matrix = jnp.stack(sketched, axis=1)
        projection = jnp.dot(sketch_matrix.T, sketch_image, precision=lax.Precision.HIGHEST)
        remainder = applied
        for index_prev in range(column + 1):
            remainder = remainder - projection[index_prev] * basis_vectors[index_prev]
        remainder_sketch = sketch_image - jnp.dot(
            sketch_matrix, projection, precision=lax.Precision.HIGHEST
        )
        new_norm = jnp.sqrt(jnp.sum(remainder_sketch * remainder_sketch))
        basis_vectors.append(remainder / new_norm)
        sketched.append(remainder_sketch / new_norm)
        entries = jnp.concatenate(
            [projection, new_norm[None], jnp.zeros((ITERS - column - 1,), jnp.float32)]
        )
        columns.append(entries)
    hessenberg = jnp.stack(columns, axis=1)
    coeffs = solve_small(hessenberg, beta_norm)
    solution = jnp.zeros_like(right_side)
    for column in range(ITERS):
        solution = solution + coeffs[column] * basis_vectors[column]
    padded = padded_2(solution, (("gx", 0), ("gy", 1)), 1)
    residual = right_side - stencil(padded, solution, drift_x, drift_y)
    return (solution, residual)


def solution(mesh):
    in_specs = (P("gx", "gy"), P("gx", "gy"), P("gx", "gy"), P(None, "gx"), P(None, "gy"))
    out_specs = (P("gx", "gy"), P("gx", "gy"))
    return jax.shard_map(body, mesh=mesh, in_specs=in_specs, out_specs=out_specs, check_vma=False)
```

profile of v0, /device:TPU:1, one launch (start us, length us, event | category | flops | bytes accessed | tf_op | source)
XLA Modules:
  0.0 370.7 jit_solution(15757160799951034432)
XLA Ops:
  0.6 1.0 copy-done
  1.7 2.3 convolution_bitcast_fusion.4
  4.3 40.5 %psum.35 = f32[256]{0:T(256)S(1)} all-reduce(f32[256]{0:T(256)S(1)} %multiply_reduce_fusion.4), channel_id=1, replica_groups=mesh['gx'=4,'gy'=8] {'gx','gy'}, use_global_device_ids=true, to_apply=%region_0.0 | all-reduce | flops 256 | bytes 2048 | tf_op jit(solution)/shard_map/psum | solution.py:68
  46.3 3.3 collective-permute-start
  49.6 1.3 collective-permute-start.1
  50.9 3.0 collective-permute-done.1
  54.1 6.7 %collective-permute-start.2 = (f32[514,1]{1,0:T(8,128)S(1)}, f32[514,1]{1,0:T(8,128)S(1)}, u32[]{:S(2)}, u32[]{:S(2)}) collective-permute-start(f32[514,1]{1,0:T(8,128)S(1)} %get-tuple-element.16), channel_id=1, source_target_pairs={{0,1},{1,2},{2,3},{3,4},{4,5},{5,6},{6,7},{8,9},{9,10},{10,11},{11... | collective-permute-start | bytes 6176 | tf_op jit(solution)/shard_map/ppermute | solution.py:18
  60.8 1.9 collective-permute-start.3
  62.7 1.4 collective-permute-done.2
  64.1 4.5 %collective-permute-done.3 = f32[514,1]{1,0:T(8,128)S(1)} collective-permute-done((f32[514,1]{1,0:T(8,128)S(1)}, f32[514,1]{1,0:T(8,128)S(1)}, u32[]{:S(2)}, u32[]{:S(2)}) %collective-permute-start.3) | collective-permute-done | bytes 2088 | tf_op jit(solution)/shard_map/ppermute | solution.py:20
  68.6 0.8 fusion.42
  69.5 1.0 copy-done.17
  70.4 1.0 convolution_bitcast_fusion.3
  71.8 38.4 %psum.36 = f32[256]{0:T(256)S(1)} all-reduce(f32[256]{0:T(256)S(1)} %multiply_reduce_fusion.3), channel_id=1, replica_groups=mesh['gx'=4,'gy'=8] {'gx','gy'}, use_global_device_ids=true, to_apply=%region_2.0 | all-reduce | flops 256 | bytes 2048 | tf_op jit(solution)/shard_map/psum | solution.py:68
  110.8 1.3 multiply_reduce_fusion.9
  112.8 2.2 subtract_divide_fusion.2
  115.0 2.4 collective-permute-start.4
  117.4 1.3 collective-permute-start.5
  119.3 2.4 collective-permute-done.5
  121.8 6.7 %collective-permute-start.6 = (f32[514,1]{1,0:T(8,128)S(1)}, f32[514,1]{1,0:T(8,128)S(1)}, u32[]{:S(2)}, u32[]{:S(2)}) collective-permute-start(f32[514,1]{1,0:T(8,128)S(1)} %get-tuple-element.14), channel_id=1, source_target_pairs={{0,1},{1,2},{2,3},{3,4},{4,5},{5,6},{6,7},{8,9},{9,10},{10,11},{11... | collective-permute-start | bytes 6176 | tf_op jit(solution)/shard_map/ppermute | solution.py:18
  128.6 1.9 collective-permute-start.7
  131.9 4.5 %collective-permute-done.7 = f32[514,1]{1,0:T(8,128)S(1)} collective-permute-done((f32[514,1]{1,0:T(8,128)S(1)}, f32[514,1]{1,0:T(8,128)S(1)}, u32[]{:S(2)}, u32[]{:S(2)}) %collective-permute-start.7) | collective-permute-done | bytes 2088 | tf_op jit(solution)/shard_map/ppermute | solution.py:20
  136.4 0.8 fusion.34
  137.2 1.0 copy-done.18
  138.2 1.8 convolution_bitcast_fusion.2
  140.0 2.0 copy.25
  142.0 1.2 multiply_reduce_fusion.2
  143.2 37.7 %psum.37 = f32[256]{0:T(256)S(1)} all-reduce(f32[256]{0:T(256)S(1)} %multiply_reduce_fusion.2), channel_id=1, replica_groups=mesh['gx'=4,'gy'=8] {'gx','gy'}, use_global_device_ids=true, to_apply=%region_4.0 | all-reduce | flops 256 | bytes 2048 | tf_op jit(solution)/shard_map/psum | solution.py:68
  183.1 2.9 subtract_divide_fusion.1
  186.0 3.1 collective-permute-start.8
  189.1 1.3 collective-permute-start.9
  190.5 3.0 collective-permute-done.9
  193.6 6.7 %collective-permute-start.10 = (f32[514,1]{1,0:T(8,128)S(1)}, f32[514,1]{1,0:T(8,128)S(1)}, u32[]{:S(2)}, u32[]{:S(2)}) collective-permute-start(f32[514,1]{1,0:T(8,128)S(1)} %get-tuple-element.12), channel_id=1, source_target_pairs={{0,1},{1,2},{2,3},{3,4},{4,5},{5,6},{6,7},{8,9},{9,10},{10,11},{11... | collective-permute-start | bytes 6176 | tf_op jit(solution)/shard_map/ppermute | solution.py:18
  200.3 2.1 collective-permute-start.11
  202.5 1.1 collective-permute-done.10
  203.7 4.5 %collective-permute-done.11 = f32[514,1]{1,0:T(8,128)S(1)} collective-permute-done((f32[514,1]{1,0:T(8,128)S(1)}, f32[514,1]{1,0:T(8,128)S(1)}, u32[]{:S(2)}, u32[]{:S(2)}) %collective-permute-start.11) | collective-permute-done | bytes 2088 | tf_op jit(solution)/shard_map/ppermute | solution.py:20
  208.1 0.8 fusion.26
  209.0 1.0 copy-done.16
  210.0 1.8 convolution_bitcast_fusion.1
  211.8 2.0 copy.30
  213.8 1.2 multiply_reduce_fusion.1
  215.0 37.8 %psum.38 = f32[256]{0:T(256)S(1)} all-reduce(f32[256]{0:T(256)S(1)} %multiply_reduce_fusion.1), channel_id=1, replica_groups=mesh['gx'=4,'gy'=8] {'gx','gy'}, use_global_device_ids=true, to_apply=%region_6.0 | all-reduce | flops 256 | bytes 2048 | tf_op jit(solution)/shard_map/psum | solution.py:68
  254.9 3.9 %subtract_divide_fusion = f32[512,512]{1,0:T(8,128)S(1)} fusion(f32[512,512]{1,0:T(8,128)} %copy-done.2, f32[512,512]{1,0:T(8,128)S(1)} %subtract_divide_fusion.2, f32[512,512]{1,0:T(8,128)} %copy-done.16, f32[]{:T(128)} %sqrt.18, f32[]{:T(128)} %bitcast.31, f32[]{:T(128)} %bitcast.30, f32[]{:T(128)} %bitcast.29, f32[512,512]{1,0:T(8,128)S(1)} %copy-done.1, ...), kind=kLoop, calls=%fused_computation.92 | loop fusion | flops 2097152 | bytes 5242900 | tf_op jit(solution)/shard_map/div | solution.py:91
  258.9 3.0 collective-permute-start.12
  261.9 1.3 collective-permute-start.13
  263.2 3.0 collective-permute-done.13
  266.4 6.7 %collective-permute-start.14 = (f32[514,1]{1,0:T(8,128)S(1)}, f32[514,1]{1,0:T(8,128)S(1)}, u32[]{:S(2)}, u32[]{:S(2)}) collective-permute-start(f32[514,1]{1,0:T(8,128)S(1)} %get-tuple-element.10), channel_id=1, source_target_pairs={{0,1},{1,2},{2,3},{3,4},{4,5},{5,6},{6,7},{8,9},{9,10},{10,11},{11... | collective-permute-start | bytes 6176 | tf_op jit(solution)/shard_map/ppermute | solution.py:18
  273.1 1.9 collective-permute-start.15
  275.1 1.3 collective-permute-done.14
  276.4 4.5 %collective-permute-done.15 = f32[514,1]{1,0:T(8,128)S(1)} collective-permute-done((f32[514,1]{1,0:T(8,128)S(1)}, f32[514,1]{1,0:T(8,128)S(1)}, u32[]{:S(2)}, u32[]{:S(2)}) %collective-permute-start.15) | collective-permute-done | bytes 2088 | tf_op jit(solution)/shard_map/ppermute | solution.py:20
  280.9 2.5 convolution_bitcast_fusion
  283.4 2.0 copy.35
  285.4 1.2 multiply_reduce_fusion
  286.6 37.8 %psum.39 = f32[256]{0:T(256)S(1)} all-reduce(f32[256]{0:T(256)S(1)} %multiply_reduce_fusion), channel_id=1, replica_groups=mesh['gx'=4,'gy'=8] {'gx','gy'}, use_global_device_ids=true, to_apply=%region_8.0 | all-reduce | flops 256 | bytes 2048 | tf_op jit(solution)/shard_map/psum | solution.py:68
  327.4 0.7 compare_reduce_fusion
  344.7 2.1 multiply_add_fusion
  346.9 2.9 collective-permute-start.16
  349.8 1.3 collective-permute-start.17
  351.1 3.0 collective-permute-done.17
  354.3 6.7 %collective-permute-start.18 = (f32[514,1]{1,0:T(8,128)S(1)}, f32[514,1]{1,0:T(8,128)S(1)}, u32[]{:S(2)}, u32[]{:S(2)}) collective-permute-start(f32[514,1]{1,0:T(8,128)S(1)} %get-tuple-element.8), channel_id=1, source_target_pairs={{0,1},{1,2},{2,3},{3,4},{4,5},{5,6},{6,7},{8,9},{9,10},{10,11},{11... | collective-permute-start | bytes 6176 | tf_op jit(solution)/shard_map/ppermute | solution.py:18
  361.0 1.9 collective-permute-start.19
  362.9 1.4 collective-permute-done.18
  364.3 4.5 %collective-permute-done.19 = f32[514,1]{1,0:T(8,128)S(1)} collective-permute-done((f32[514,1]{1,0:T(8,128)S(1)}, f32[514,1]{1,0:T(8,128)S(1)}, u32[]{:S(2)}, u32[]{:S(2)}) %collective-permute-start.19) | collective-permute-done | bytes 2088 | tf_op jit(solution)/shard_map/ppermute | solution.py:20
  368.8 1.9 fusion.2
  (87 shorter events, 11.7 us)
Async XLA Ops:
  0.6 1.0 copy-start
  1.7 2.5 copy-start.13
  4.0 42.2 %copy-start.1 = (f32[512,512]{1,0:T(8,128)S(1)}, f32[512,512]{1,0:T(8,128)}, u32[]{:S(2)}) copy-start(f32[512,512]{1,0:T(8,128)} %param.5) | copy-start | bytes 3145732
  46.2 22.4 %copy-start.8 = (f32[512,512]{1,0:T(8,128)S(1)}, f32[512,512]{1,0:T(8,128)}, u32[]{:S(2)}) copy-start(f32[512,512]{1,0:T(8,128)} %param.6) | copy-start | bytes 3145732
  46.3 22.3 %copy-start.3 = (f32[512,512]{1,0:T(8,128)S(1)}, f32[512,512]{1,0:T(8,128)}, u32[]{:S(2)}) copy-start(f32[512,512]{1,0:T(8,128)} %param.7) | copy-start | bytes 3145732
  46.3 4.6 %collective-permute-start = (f32[1,512]{1,0:T(1,128)S(1)}, f32[1,512]{1,0:T(1,128)S(1)}, u32[]{:S(2)}, u32[]{:S(2)}) collective-permute-start(f32[1,512]{1,0:T(1,128)S(1)} %get-tuple-element.26), channel_id=1, source_target_pairs={{0,8},{8,16},{16,24},{1,9},{9,17},{17,25},{2,10},{10,18},{18,26},{... | collective-permute-start | bytes 6152 | tf_op jit(solution)/shard_map/ppermute | solution.py:18
  49.6 4.3 %collective-permute-start.1 = (f32[1,512]{1,0:T(1,128)S(1)}, f32[1,512]{1,0:T(1,128)S(1)}, u32[]{:S(2)}, u32[]{:S(2)}) collective-permute-start(f32[1,512]{1,0:T(1,128)S(1)} %get-tuple-element.27), channel_id=1, source_target_pairs={{8,0},{16,8},{24,16},{9,1},{17,9},{25,17},{10,2},{18,10},{26,18},{... | collective-permute-start | bytes 6152 | tf_op jit(solution)/shard_map/ppermute | solution.py:20
  54.1 10.1 %collective-permute-start.2 = (f32[514,1]{1,0:T(8,128)S(1)}, f32[514,1]{1,0:T(8,128)S(1)}, u32[]{:S(2)}, u32[]{:S(2)}) collective-permute-start(f32[514,1]{1,0:T(8,128)S(1)} %get-tuple-element.16), channel_id=1, source_target_pairs={{0,1},{1,2},{2,3},{3,4},{4,5},{5,6},{6,7},{8,9},{9,10},{10,11},{11... | collective-permute-start | bytes 6176 | tf_op jit(solution)/shard_map/ppermute | solution.py:18
  60.8 7.8 %collective-permute-start.3 = (f32[514,1]{1,0:T(8,128)S(1)}, f32[514,1]{1,0:T(8,128)S(1)}, u32[]{:S(2)}, u32[]{:S(2)}) collective-permute-start(f32[514,1]{1,0:T(8,128)S(1)} %get-tuple-element.17), channel_id=1, source_target_pairs={{1,0},{2,1},{3,2},{4,3},{5,4},{6,5},{7,6},{9,8},{10,9},{11,10},{12... | collective-permute-start | bytes 6176 | tf_op jit(solution)/shard_map/ppermute | solution.py:20
  69.4 1.0 copy-start.17
  112.7 23.6 %copy-start.9 = (f32[512,512]{1,0:T(8,128)S(1)}, f32[512,512]{1,0:T(8,128)}, u32[]{:S(2)}) copy-start(f32[512,512]{1,0:T(8,128)} %param.6) | copy-start | bytes 3145732
  115.0 21.4 %copy-start.4 = (f32[512,512]{1,0:T(8,128)S(1)}, f32[512,512]{1,0:T(8,128)}, u32[]{:S(2)}) copy-start(f32[512,512]{1,0:T(8,128)} %param.7) | copy-start | bytes 3145732
  115.0 4.4 %collective-permute-start.4 = (f32[1,512]{1,0:T(1,128)S(1)}, f32[1,512]{1,0:T(1,128)S(1)}, u32[]{:S(2)}, u32[]{:S(2)}) collective-permute-start(f32[1,512]{1,0:T(1,128)S(1)} %get-tuple-element.24), channel_id=1, source_target_pairs={{0,8},{8,16},{16,24},{1,9},{9,17},{17,25},{2,10},{10,18},{18,26},{... | collective-permute-start | bytes 6152 | tf_op jit(solution)/shard_map/ppermute | solution.py:18
  117.4 4.3 %collective-permute-start.5 = (f32[1,512]{1,0:T(1,128)S(1)}, f32[1,512]{1,0:T(1,128)S(1)}, u32[]{:S(2)}, u32[]{:S(2)}) collective-permute-start(f32[1,512]{1,0:T(1,128)S(1)} %get-tuple-element.25), channel_id=1, source_target_pairs={{8,0},{16,8},{24,16},{9,1},{17,9},{25,17},{10,2},{18,10},{26,18},{... | collective-permute-start | bytes 6152 | tf_op jit(solution)/shard_map/ppermute | solution.py:20
  121.8 10.1 %collective-permute-start.6 = (f32[514,1]{1,0:T(8,128)S(1)}, f32[514,1]{1,0:T(8,128)S(1)}, u32[]{:S(2)}, u32[]{:S(2)}) collective-permute-start(f32[514,1]{1,0:T(8,128)S(1)} %get-tuple-element.14), channel_id=1, source_target_pairs={{0,1},{1,2},{2,3},{3,4},{4,5},{5,6},{6,7},{8,9},{9,10},{10,11},{11... | collective-permute-start | bytes 6176 | tf_op jit(solution)/shard_map/ppermute | solution.py:18
  128.6 7.8 %collective-permute-start.7 = (f32[514,1]{1,0:T(8,128)S(1)}, f32[514,1]{1,0:T(8,128)S(1)}, u32[]{:S(2)}, u32[]{:S(2)}) collective-permute-start(f32[514,1]{1,0:T(8,128)S(1)} %get-tuple-element.15), channel_id=1, source_target_pairs={{1,0},{2,1},{3,2},{4,3},{5,4},{6,5},{7,6},{9,8},{10,9},{11,10},{12... | collective-permute-start | bytes 6176 | tf_op jit(solution)/shard_map/ppermute | solution.py:20
  137.2 1.0 copy-start.18
  183.1 25.1 %copy-start.10 = (f32[512,512]{1,0:T(8,128)S(1)}, f32[512,512]{1,0:T(8,128)}, u32[]{:S(2)}) copy-start(f32[512,512]{1,0:T(8,128)} %param.6) | copy-start | bytes 3145732
  186.0 23.0 %copy-start.2 = (f32[512,512]{1,0:T(8,128)}, f32[512,512]{1,0:T(8,128)S(1)}, u32[]{:S(2)}) copy-start(f32[512,512]{1,0:T(8,128)S(1)} %subtract_divide_fusion.1) | copy-start | bytes 3145732
  186.0 22.1 %copy-start.5 = (f32[512,512]{1,0:T(8,128)S(1)}, f32[512,512]{1,0:T(8,128)}, u32[]{:S(2)}) copy-start(f32[512,512]{1,0:T(8,128)} %param.7) | copy-start | bytes 3145732
  186.0 4.4 %collective-permute-start.8 = (f32[1,512]{1,0:T(1,128)S(1)}, f32[1,512]{1,0:T(1,128)S(1)}, u32[]{:S(2)}, u32[]{:S(2)}) collective-permute-start(f32[1,512]{1,0:T(1,128)S(1)} %get-tuple-element.22), channel_id=1, source_target_pairs={{0,8},{8,16},{16,24},{1,9},{9,17},{17,25},{2,10},{10,18},{18,26},{... | collective-permute-start | bytes 6152 | tf_op jit(solution)/shard_map/ppermute | solution.py:18
  189.1 4.3 %collective-permute-start.9 = (f32[1,512]{1,0:T(1,128)S(1)}, f32[1,512]{1,0:T(1,128)S(1)}, u32[]{:S(2)}, u32[]{:S(2)}) collective-permute-start(f32[1,512]{1,0:T(1,128)S(1)} %get-tuple-element.23), channel_id=1, source_target_pairs={{8,0},{16,8},{24,16},{9,1},{17,9},{25,17},{10,2},{18,10},{26,18},{... | collective-permute-start | bytes 6152 | tf_op jit(solution)/shard_map/ppermute | solution.py:20
  193.6 10.1 %collective-permute-start.10 = (f32[514,1]{1,0:T(8,128)S(1)}, f32[514,1]{1,0:T(8,128)S(1)}, u32[]{:S(2)}, u32[]{:S(2)}) collective-permute-start(f32[514,1]{1,0:T(8,128)S(1)} %get-tuple-element.12), channel_id=1, source_target_pairs={{0,1},{1,2},{2,3},{3,4},{4,5},{5,6},{6,7},{8,9},{9,10},{10,11},{11... | collective-permute-start | bytes 6176 | tf_op jit(solution)/shard_map/ppermute | solution.py:18
  200.3 7.8 %collective-permute-start.11 = (f32[514,1]{1,0:T(8,128)S(1)}, f32[514,1]{1,0:T(8,128)S(1)}, u32[]{:S(2)}, u32[]{:S(2)}) collective-permute-start(f32[514,1]{1,0:T(8,128)S(1)} %get-tuple-element.13), channel_id=1, source_target_pairs={{1,0},{2,1},{3,2},{4,3},{5,4},{6,5},{7,6},{9,8},{10,9},{11,10},{12... | collective-permute-start | bytes 6176 | tf_op jit(solution)/shard_map/ppermute | solution.py:20
  209.0 1.0 copy-start.16
  254.9 26.0 %copy-start.11 = (f32[512,512]{1,0:T(8,128)S(1)}, f32[512,512]{1,0:T(8,128)}, u32[]{:S(2)}) copy-start(f32[512,512]{1,0:T(8,128)} %param.6) | copy-start | bytes 3145732
  258.8 22.0 %copy-start.14 = (f32[512,512]{1,0:T(8,128)}, f32[512,512]{1,0:T(8,128)S(1)}, u32[]{:S(2)}) copy-start(f32[512,512]{1,0:T(8,128)S(1)} %subtract_divide_fusion) | copy-start | bytes 3145732
  258.9 22.0 %copy-start.6 = (f32[512,512]{1,0:T(8,128)S(1)}, f32[512,512]{1,0:T(8,128)}, u32[]{:S(2)}) copy-start(f32[512,512]{1,0:T(8,128)} %param.7) | copy-start | bytes 3145732
  258.9 4.3 %collective-permute-start.12 = (f32[1,512]{1,0:T(1,128)S(1)}, f32[1,512]{1,0:T(1,128)S(1)}, u32[]{:S(2)}, u32[]{:S(2)}) collective-permute-start(f32[1,512]{1,0:T(1,128)S(1)} %get-tuple-element.20), channel_id=1, source_target_pairs={{0,8},{8,16},{16,24},{1,9},{9,17},{17,25},{2,10},{10,18},{18,26},{... | collective-permute-start | bytes 6152 | tf_op jit(solution)/shard_map/ppermute | solution.py:18
  261.9 4.3 %collective-permute-start.13 = (f32[1,512]{1,0:T(1,128)S(1)}, f32[1,512]{1,0:T(1,128)S(1)}, u32[]{:S(2)}, u32[]{:S(2)}) collective-permute-start(f32[1,512]{1,0:T(1,128)S(1)} %get-tuple-element.21), channel_id=1, source_target_pairs={{8,0},{16,8},{24,16},{9,1},{17,9},{25,17},{10,2},{18,10},{26,18},{... | collective-permute-start | bytes 6152 | tf_op jit(solution)/shard_map/ppermute | solution.py:20
  266.4 10.1 %collective-permute-start.14 = (f32[514,1]{1,0:T(8,128)S(1)}, f32[514,1]{1,0:T(8,128)S(1)}, u32[]{:S(2)}, u32[]{:S(2)}) collective-permute-start(f32[514,1]{1,0:T(8,128)S(1)} %get-tuple-element.10), channel_id=1, source_target_pairs={{0,1},{1,2},{2,3},{3,4},{4,5},{5,6},{6,7},{8,9},{9,10},{10,11},{11... | collective-permute-start | bytes 6176 | tf_op jit(solution)/shard_map/ppermute | solution.py:18
  273.1 7.8 %collective-permute-start.15 = (f32[514,1]{1,0:T(8,128)S(1)}, f32[514,1]{1,0:T(8,128)S(1)}, u32[]{:S(2)}, u32[]{:S(2)}) collective-permute-start(f32[514,1]{1,0:T(8,128)S(1)} %get-tuple-element.11), channel_id=1, source_target_pairs={{1,0},{2,1},{3,2},{4,3},{5,4},{6,5},{7,6},{9,8},{10,9},{11,10},{12... | collective-permute-start | bytes 6176 | tf_op jit(solution)/shard_map/ppermute | solution.py:20
  344.7 24.1 %copy-start.12 = (f32[512,512]{1,0:T(8,128)S(1)}, f32[512,512]{1,0:T(8,128)}, u32[]{:S(2)}) copy-start(f32[512,512]{1,0:T(8,128)} %param.6) | copy-start | bytes 3145732
  346.8 23.9 %copy-start.15 = (f32[512,512]{1,0:T(8,128)}, f32[512,512]{1,0:T(8,128)S(1)}, u32[]{:S(2)}) copy-start(f32[512,512]{1,0:T(8,128)S(1)} %multiply_add_fusion) | copy-start | bytes 3145732
  346.8 22.0 %copy-start.7 = (f32[512,512]{1,0:T(8,128)S(1)}, f32[512,512]{1,0:T(8,128)}, u32[]{:S(2)}) copy-start(f32[512,512]{1,0:T(8,128)} %param.7) | copy-start | bytes 3145732
  346.9 4.2 %collective-permute-start.16 = (f32[1,512]{1,0:T(1,128)S(1)}, f32[1,512]{1,0:T(1,128)S(1)}, u32[]{:S(2)}, u32[]{:S(2)}) collective-permute-start(f32[1,512]{1,0:T(1,128)S(1)} %get-tuple-element.18), channel_id=1, source_target_pairs={{0,8},{8,16},{16,24},{1,9},{9,17},{17,25},{2,10},{10,18},{18,26},{... | collective-permute-start | bytes 6152 | tf_op jit(solution)/shard_map/ppermute | solution.py:18
  349.8 4.3 %collective-permute-start.17 = (f32[1,512]{1,0:T(1,128)S(1)}, f32[1,512]{1,0:T(1,128)S(1)}, u32[]{:S(2)}, u32[]{:S(2)}) collective-permute-start(f32[1,512]{1,0:T(1,128)S(1)} %get-tuple-element.19), channel_id=1, source_target_pairs={{8,0},{16,8},{24,16},{9,1},{17,9},{25,17},{10,2},{18,10},{26,18},{... | collective-permute-start | bytes 6152 | tf_op jit(solution)/shard_map/ppermute | solution.py:20
  354.3 10.1 %collective-permute-start.18 = (f32[514,1]{1,0:T(8,128)S(1)}, f32[514,1]{1,0:T(8,128)S(1)}, u32[]{:S(2)}, u32[]{:S(2)}) collective-permute-start(f32[514,1]{1,0:T(8,128)S(1)} %get-tuple-element.8), channel_id=1, source_target_pairs={{0,1},{1,2},{2,3},{3,4},{4,5},{5,6},{6,7},{8,9},{9,10},{10,11},{11... | collective-permute-start | bytes 6176 | tf_op jit(solution)/shard_map/ppermute | solution.py:18
  361.0 7.8 %collective-permute-start.19 = (f32[514,1]{1,0:T(8,128)S(1)}, f32[514,1]{1,0:T(8,128)S(1)}, u32[]{:S(2)}, u32[]{:S(2)}) collective-permute-start(f32[514,1]{1,0:T(8,128)S(1)} %get-tuple-element.9), channel_id=1, source_target_pairs={{1,0},{2,1},{3,2},{4,3},{5,4},{6,5},{7,6},{9,8},{10,9},{11,10},{12... | collective-permute-start | bytes 6176 | tf_op jit(solution)/shard_map/ppermute | solution.py:20
where the time goes:
time: 372 us; the launch traced here: 371 us
  blocking collectives  192 us (52%)
  starting transfers between devices  64.4 us (17%)
  waiting for transfers between devices  42.7 us (11%)
  other arithmetic  28.1 us (8%)
  between operations  19.8 us (5%)
  local copies, waits for them, and re-layouts  13.1 us (4%)
  matrix products  10.4 us (3%)
    psum x5, blocking collectives, sketch(): return lax.psum(partial_value, ('gx', 'gy'))  192 us
    ppermute x10, starting transfers between devices, padded_2(): lax.ppermute(tail, axis, [(i, (i + 1) % count) for i in range(ends)])  48.2 us
    ppermute x10, waiting for transfers between devices, padded_2(): lax.ppermute(head, axis, [((i + 1) % count, i) for i in range(ends)])  36.7 us
    ppermute x10, starting transfers between devices, padded_2(): lax.ppermute(head, axis, [((i + 1) % count, i) for i in range(ends)])  16.2 us
    unnamed x43, local copies, waits for them, and re-layouts  10.5 us
    dot_general x5, matrix products, sketch(): product = jnp.dot(field, sketch_cols.T, precision=lax.Precision.HIGHEST)  9.45 us
    div x3, other arithmetic, body(): basis_vectors.append(remainder / new_norm)  9.05 us
  transfers between devices with their start and end apart: 20, of which 15 were waited for; matrix products, arithmetic and copies ran while one was open for 0% of the time, Pallas kernels for 0%

commit v1 on v0

--- a/solution.py
+++ b/solution.py
@@ -61,11 +61,19 @@
 def body(right_side, drift_x, drift_y, sketch_rows, sketch_cols):
 
     def sketch(field):
+
+        def rest_the_ends(load):
+            group_axis = "gx"
+            along_axis = "gy"
+            for dev_i in (along_axis, group_axis):
+                load = jax.lax.psum(load, dev_i)
+            return load
+
         product = jnp.dot(field, sketch_cols.T, precision=lax.Precision.HIGHEST)
         partial_value = jnp.einsum(
             "ki,ik->k", sketch_rows, product, precision=lax.Precision.HIGHEST
         )
-        return lax.psum(partial_value, ("gx", "gy"))
+        return rest_the_ends(partial_value)
 
     first_sketch = sketch(right_side)
     beta_norm = jnp.sqrt(jnp.sum(first_sketch * first_sketch))

time: 372 us -> 287 us (0.77)
  blocking collectives: 192 us -> 91.2 us
  waiting for transfers between devices: 42.7 us -> 54 us
  starting transfers between devices: 64.4 us -> 68.4 us
    psum x5 -> x10, blocking collectives: 192 us -> 91.2 us  [rest_the_ends(): load = jax.lax.psum(load, dev_i)]
    ppermute x10, waiting for transfers between devices: 36.7 us -> 48.7 us  [padded_2(): lax.ppermute(head, axis, [((i + 1) % count, i) for i in range(ends)])]
  transfers between devices with their start and end apart: 20 -> 20, of which waited for: 15 -> 15; matrix products, arithmetic and copies ran while one was open for 0% -> 1% of each run, Pallas kernels for 0% -> 0%
where the time goes in v1:
time: 287 us; the launch traced here: 285 us
  blocking collectives  91.2 us (32%)
  starting transfers between devices  68.4 us (24%)
  waiting for transfers between devices  54 us (19%)
  other arithmetic  28 us (10%)
  between operations  19.9 us (7%)
  local copies, waits for them, and re-layouts  13.2 us (5%)
  matrix products  10.4 us (4%)
    psum x10, blocking collectives, rest_the_ends(): load = jax.lax.psum(load, dev_i)  91.2 us
    ppermute x10, starting transfers between devices, padded_2(): lax.ppermute(tail, axis, [(i, (i + 1) % count) for i in range(ends)])  51.4 us
    ppermute x10, waiting for transfers between devices, padded_2(): lax.ppermute(head, axis, [((i + 1) % count, i) for i in range(ends)])  48.7 us
    ppermute x10, starting transfers between devices, padded_2(): lax.ppermute(head, axis, [((i + 1) % count, i) for i in range(ends)])  17 us
    unnamed x43, local copies, waits for them, and re-layouts  10.6 us
    dot_general x5, matrix products, sketch(): product = jnp.dot(field, sketch_cols.T, precision=lax.Precision.HIGHEST)  9.44 us
    div x3, other arithmetic, body(): basis_vectors.append(remainder / new_norm)  9.1 us
  transfers between devices with their start and end apart: 20, of which 15 were waited for; matrix products, arithmetic and copies ran while one was open for 1% of the time, Pallas kernels for 0%

profile of v1, /device:TPU:1, one launch (start us, length us, event | category | flops | bytes accessed | tf_op | source)
XLA Modules:
  0.0 285.2 jit_solution(1362355741394492905)
XLA Ops:
  0.6 1.0 copy-done
  1.7 2.3 convolution_bitcast_fusion.4
  4.3 12.6 %psum.70 = f32[256]{0:T(256)S(1)} all-reduce(f32[256]{0:T(256)S(1)} %multiply_reduce_fusion.4), channel_id=1, replica_groups=mesh['gx'=4,'gy'=8] {'gy'}, use_global_device_ids=true, to_apply=%region_0.0 | all-reduce | flops 256 | bytes 2048 | tf_op jit(solution)/shard_map/psum | solution.py:69
  16.9 10.0 %psum.71 = f32[256]{0:T(256)S(1)} all-reduce(f32[256]{0:T(256)S(1)} %psum.70), channel_id=1, replica_groups=mesh['gx'=4,'gy'=8] {'gx'}, use_global_device_ids=true, to_apply=%region_1.0 | all-reduce | flops 256 | bytes 2048 | tf_op jit(solution)/shard_map/psum | solution.py:69
  28.4 1.4 collective-permute-start
  29.8 1.3 collective-permute-start.1
  31.1 3.0 %collective-permute-done.1 = f32[1,512]{1,0:T(1,128)S(1)} collective-permute-done((f32[1,512]{1,0:T(1,128)S(1)}, f32[1,512]{1,0:T(1,128)S(1)}, u32[]{:S(2)}, u32[]{:S(2)}) %collective-permute-start.1) | collective-permute-done | bytes 2080 | tf_op jit(solution)/shard_map/ppermute | solution.py:20
  34.3 6.1 %collective-permute-start.2 = (f32[514,1]{1,0:T(8,128)S(1)}, f32[514,1]{1,0:T(8,128)S(1)}, u32[]{:S(2)}, u32[]{:S(2)}) collective-permute-start(f32[514,1]{1,0:T(8,128)S(1)} %get-tuple-element.16), channel_id=1, source_target_pairs={{0,1},{1,2},{2,3},{3,4},{4,5},{5,6},{6,7},{8,9},{9,10},{10,11},{11... | collective-permute-start | bytes 6176 | tf_op jit(solution)/shard_map/ppermute | solution.py:18
  40.4 2.8 collective-permute-start.3
  43.7 6.1 %collective-permute-done.3 = f32[514,1]{1,0:T(8,128)S(1)} collective-permute-done((f32[514,1]{1,0:T(8,128)S(1)}, f32[514,1]{1,0:T(8,128)S(1)}, u32[]{:S(2)}, u32[]{:S(2)}) %collective-permute-start.3) | collective-permute-done | bytes 2088 | tf_op jit(solution)/shard_map/ppermute | solution.py:20
  50.7 1.0 copy-done.17
  51.6 1.0 convolution_bitcast_fusion.3
  53.0 10.4 %psum.72 = f32[256]{0:T(256)S(1)} all-reduce(f32[256]{0:T(256)S(1)} %multiply_reduce_fusion.3), channel_id=1, replica_groups=mesh['gx'=4,'gy'=8] {'gy'}, use_global_device_ids=true, to_apply=%region_3.0 | all-reduce | flops 256 | bytes 2048 | tf_op jit(solution)/shard_map/psum | solution.py:69
  63.4 7.1 %psum.73 = f32[256]{0:T(256)S(1)} all-reduce(f32[256]{0:T(256)S(1)} %psum.72), channel_id=1, replica_groups=mesh['gx'=4,'gy'=8] {'gx'}, use_global_device_ids=true, to_apply=%region_4.0 | all-reduce | flops 256 | bytes 2048 | tf_op jit(solution)/shard_map/psum | solution.py:69
  71.1 1.3 multiply_reduce_fusion.9
  73.2 2.2 subtract_divide_fusion.2
  75.4 2.9 %collective-permute-start.4 = (f32[1,512]{1,0:T(1,128)S(1)}, f32[1,512]{1,0:T(1,128)S(1)}, u32[]{:S(2)}, u32[]{:S(2)}) collective-permute-start(f32[1,512]{1,0:T(1,128)S(1)} %get-tuple-element.24), channel_id=1, source_target_pairs={{0,8},{8,16},{16,24},{1,9},{9,17},{17,25},{2,10},{10,18},{18,26},{... | collective-permute-start | bytes 6152 | tf_op jit(solution)/shard_map/ppermute | solution.py:18
  78.4 1.3 collective-permute-start.5
  80.3 2.4 collective-permute-done.5
  82.9 7.7 %collective-permute-start.6 = (f32[514,1]{1,0:T(8,128)S(1)}, f32[514,1]{1,0:T(8,128)S(1)}, u32[]{:S(2)}, u32[]{:S(2)}) collective-permute-start(f32[514,1]{1,0:T(8,128)S(1)} %get-tuple-element.14), channel_id=1, source_target_pairs={{0,1},{1,2},{2,3},{3,4},{4,5},{5,6},{6,7},{8,9},{9,10},{10,11},{11... | collective-permute-start | bytes 6176 | tf_op jit(solution)/shard_map/ppermute | solution.py:18
  90.5 1.9 collective-permute-start.7
  93.9 7.1 %collective-permute-done.7 = f32[514,1]{1,0:T(8,128)S(1)} collective-permute-done((f32[514,1]{1,0:T(8,128)S(1)}, f32[514,1]{1,0:T(8,128)S(1)}, u32[]{:S(2)}, u32[]{:S(2)}) %collective-permute-start.7) | collective-permute-done | bytes 2088 | tf_op jit(solution)/shard_map/ppermute | solution.py:20
  101.8 1.0 copy-done.18
  102.7 1.8 convolution_bitcast_fusion.2
  104.5 2.0 copy.25
  106.6 1.2 multiply_reduce_fusion.2
  107.7 10.4 %psum.74 = f32[256]{0:T(256)S(1)} all-reduce(f32[256]{0:T(256)S(1)} %multiply_reduce_fusion.2), channel_id=1, replica_groups=mesh['gx'=4,'gy'=8] {'gy'}, use_global_device_ids=true, to_apply=%region_6.0 | all-reduce | flops 256 | bytes 2048 | tf_op jit(solution)/shard_map/psum | solution.py:69
  118.1 6.6 %psum.75 = f32[256]{0:T(256)S(1)} all-reduce(f32[256]{0:T(256)S(1)} %psum.74), channel_id=1, replica_groups=mesh['gx'=4,'gy'=8] {'gx'}, use_global_device_ids=true, to_apply=%region_7.0 | all-reduce | flops 256 | bytes 2048 | tf_op jit(solution)/shard_map/psum | solution.py:69
  126.9 2.9 %subtract_divide_fusion.1 = f32[512,512]{1,0:T(8,128)S(1)} fusion(f32[512,512]{1,0:T(8,128)S(1)} %subtract_divide_fusion.2, f32[512,512]{1,0:T(8,128)} %copy-done.18, f32[]{:T(128)} %sqrt.17, f32[]{:T(128)} %bitcast.20, f32[]{:T(128)} %bitcast.19, f32[512,512]{1,0:T(8,128)S(1)} %copy-done.1, f32[]{:T(128)S(6)} %sqrt.15), kind=kLoop, calls=%fused_computation.93 | loop fusion | flops 1572864 | bytes 4194320 | tf_op jit(solution)/shard_map/div | solution.py:99
  129.9 3.4 %collective-permute-start.8 = (f32[1,512]{1,0:T(1,128)S(1)}, f32[1,512]{1,0:T(1,128)S(1)}, u32[]{:S(2)}, u32[]{:S(2)}) collective-permute-start(f32[1,512]{1,0:T(1,128)S(1)} %get-tuple-element.22), channel_id=1, source_target_pairs={{0,8},{8,16},{16,24},{1,9},{9,17},{17,25},{2,10},{10,18},{18,26},{... | collective-permute-start | bytes 6152 | tf_op jit(solution)/shard_map/ppermute | solution.py:18
  133.4 1.3 collective-permute-start.9
  134.7 3.0 %collective-permute-done.9 = f32[1,512]{1,0:T(1,128)S(1)} collective-permute-done((f32[1,512]{1,0:T(1,128)S(1)}, f32[1,512]{1,0:T(1,128)S(1)}, u32[]{:S(2)}, u32[]{:S(2)}) %collective-permute-start.9) | collective-permute-done | bytes 2080 | tf_op jit(solution)/shard_map/ppermute | solution.py:20
  137.8 7.7 %collective-permute-start.10 = (f32[514,1]{1,0:T(8,128)S(1)}, f32[514,1]{1,0:T(8,128)S(1)}, u32[]{:S(2)}, u32[]{:S(2)}) collective-permute-start(f32[514,1]{1,0:T(8,128)S(1)} %get-tuple-element.12), channel_id=1, source_target_pairs={{0,1},{1,2},{2,3},{3,4},{4,5},{5,6},{6,7},{8,9},{9,10},{10,11},{11... | collective-permute-start | bytes 6176 | tf_op jit(solution)/shard_map/ppermute | solution.py:18
  145.5 1.9 collective-permute-start.11
  147.5 1.3 collective-permute-done.10
  148.8 7.1 %collective-permute-done.11 = f32[514,1]{1,0:T(8,128)S(1)} collective-permute-done((f32[514,1]{1,0:T(8,128)S(1)}, f32[514,1]{1,0:T(8,128)S(1)}, u32[]{:S(2)}, u32[]{:S(2)}) %collective-permute-start.11) | collective-permute-done | bytes 2088 | tf_op jit(solution)/shard_map/ppermute | solution.py:20
  156.8 1.0 copy-done.16
  157.7 1.8 convolution_bitcast_fusion.1
  159.5 2.1 copy.30
  161.6 1.2 multiply_reduce_fusion.1
  162.8 10.4 %psum.76 = f32[256]{0:T(256)S(1)} all-reduce(f32[256]{0:T(256)S(1)} %multiply_reduce_fusion.1), channel_id=1, replica_groups=mesh['gx'=4,'gy'=8] {'gy'}, use_global_device_ids=true, to_apply=%region_9.0 | all-reduce | flops 256 | bytes 2048 | tf_op jit(solution)/shard_map/psum | solution.py:69
  173.1 6.8 %psum.77 = f32[256]{0:T(256)S(1)} all-reduce(f32[256]{0:T(256)S(1)} %psum.76), channel_id=1, replica_groups=mesh['gx'=4,'gy'=8] {'gx'}, use_global_device_ids=true, to_apply=%region_10.0 | all-reduce | flops 256 | bytes 2048 | tf_op jit(solution)/shard_map/psum | solution.py:69
  182.1 4.0 %subtract_divide_fusion = f32[512,512]{1,0:T(8,128)S(1)} fusion(f32[512,512]{1,0:T(8,128)} %copy-done.2, f32[512,512]{1,0:T(8,128)S(1)} %subtract_divide_fusion.2, f32[512,512]{1,0:T(8,128)} %copy-done.16, f32[]{:T(128)} %sqrt.18, f32[]{:T(128)} %bitcast.31, f32[]{:T(128)} %bitcast.30, f32[]{:T(128)} %bitcast.29, f32[512,512]{1,0:T(8,128)S(1)} %copy-done.1, ...), kind=kLoop, calls=%fused_computation.92 | loop fusion | flops 2097152 | bytes 5242900 | tf_op jit(solution)/shard_map/div | solution.py:99
  186.1 3.4 %collective-permute-start.12 = (f32[1,512]{1,0:T(1,128)S(1)}, f32[1,512]{1,0:T(1,128)S(1)}, u32[]{:S(2)}, u32[]{:S(2)}) collective-permute-start(f32[1,512]{1,0:T(1,128)S(1)} %get-tuple-element.20), channel_id=1, source_target_pairs={{0,8},{8,16},{16,24},{1,9},{9,17},{17,25},{2,10},{10,18},{18,26},{... | collective-permute-start | bytes 6152 | tf_op jit(solution)/shard_map/ppermute | solution.py:18
  189.5 1.3 collective-permute-start.13
  190.9 3.0 %collective-permute-done.13 = f32[1,512]{1,0:T(1,128)S(1)} collective-permute-done((f32[1,512]{1,0:T(1,128)S(1)}, f32[1,512]{1,0:T(1,128)S(1)}, u32[]{:S(2)}, u32[]{:S(2)}) %collective-permute-start.13) | collective-permute-done | bytes 2080 | tf_op jit(solution)/shard_map/ppermute | solution.py:20
  194.0 7.7 %collective-permute-start.14 = (f32[514,1]{1,0:T(8,128)S(1)}, f32[514,1]{1,0:T(8,128)S(1)}, u32[]{:S(2)}, u32[]{:S(2)}) collective-permute-start(f32[514,1]{1,0:T(8,128)S(1)} %get-tuple-element.10), channel_id=1, source_target_pairs={{0,1},{1,2},{2,3},{3,4},{4,5},{5,6},{6,7},{8,9},{9,10},{10,11},{11... | collective-permute-start | bytes 6176 | tf_op jit(solution)/shard_map/ppermute | solution.py:18
  201.7 1.9 collective-permute-start.15
  203.7 1.3 collective-permute-done.14
  205.0 7.1 %collective-permute-done.15 = f32[514,1]{1,0:T(8,128)S(1)} collective-permute-done((f32[514,1]{1,0:T(8,128)S(1)}, f32[514,1]{1,0:T(8,128)S(1)}, u32[]{:S(2)}, u32[]{:S(2)}) %collective-permute-start.15) | collective-permute-done | bytes 2088 | tf_op jit(solution)/shard_map/ppermute | solution.py:20
  212.1 2.5 convolution_bitcast_fusion
  214.6 2.1 copy.35
  216.6 1.2 multiply_reduce_fusion
  217.8 10.4 %psum.78 = f32[256]{0:T(256)S(1)} all-reduce(f32[256]{0:T(256)S(1)} %multiply_reduce_fusion), channel_id=1, replica_groups=mesh['gx'=4,'gy'=8] {'gy'}, use_global_device_ids=true, to_apply=%region_12.0 | all-reduce | flops 256 | bytes 2048 | tf_op jit(solution)/shard_map/psum | solution.py:69
  228.2 6.6 %psum.79 = f32[256]{0:T(256)S(1)} all-reduce(f32[256]{0:T(256)S(1)} %psum.78), channel_id=1, replica_groups=mesh['gx'=4,'gy'=8] {'gx'}, use_global_device_ids=true, to_apply=%region_13.0 | all-reduce | flops 256 | bytes 2048 | tf_op jit(solution)/shard_map/psum | solution.py:69
  255.1 2.1 multiply_add_fusion
  257.3 3.4 %collective-permute-start.16 = (f32[1,512]{1,0:T(1,128)S(1)}, f32[1,512]{1,0:T(1,128)S(1)}, u32[]{:S(2)}, u32[]{:S(2)}) collective-permute-start(f32[1,512]{1,0:T(1,128)S(1)} %get-tuple-element.18), channel_id=1, source_target_pairs={{0,8},{8,16},{16,24},{1,9},{9,17},{17,25},{2,10},{10,18},{18,26},{... | collective-permute-start | bytes 6152 | tf_op jit(solution)/shard_map/ppermute | solution.py:18
  260.7 1.3 collective-permute-start.17
  262.0 3.0 %collective-permute-done.17 = f32[1,512]{1,0:T(1,128)S(1)} collective-permute-done((f32[1,512]{1,0:T(1,128)S(1)}, f32[1,512]{1,0:T(1,128)S(1)}, u32[]{:S(2)}, u32[]{:S(2)}) %collective-permute-start.17) | collective-permute-done | bytes 2080 | tf_op jit(solution)/shard_map/ppermute | solution.py:20
  265.2 7.7 %collective-permute-start.18 = (f32[514,1]{1,0:T(8,128)S(1)}, f32[514,1]{1,0:T(8,128)S(1)}, u32[]{:S(2)}, u32[]{:S(2)}) collective-permute-start(f32[514,1]{1,0:T(8,128)S(1)} %get-tuple-element.8), channel_id=1, source_target_pairs={{0,1},{1,2},{2,3},{3,4},{4,5},{5,6},{6,7},{8,9},{9,10},{10,11},{11... | collective-permute-start | bytes 6176 | tf_op jit(solution)/shard_map/ppermute | solution.py:18
  272.9 1.9 collective-permute-start.19
  274.8 1.4 collective-permute-done.18
  276.2 7.1 %collective-permute-done.19 = f32[514,1]{1,0:T(8,128)S(1)} collective-permute-done((f32[514,1]{1,0:T(8,128)S(1)}, f32[514,1]{1,0:T(8,128)S(1)}, u32[]{:S(2)}, u32[]{:S(2)}) %collective-permute-start.19) | collective-permute-done | bytes 2088 | tf_op jit(solution)/shard_map/ppermute | solution.py:20
  283.3 1.9 fusion.2
  (92 shorter events, 15.4 us)
Async XLA Ops:
  0.6 1.0 copy-start
  1.7 2.5 copy-start.13
  4.0 24.2 %copy-start.1 = (f32[512,512]{1,0:T(8,128)S(1)}, f32[512,512]{1,0:T(8,128)}, u32[]{:S(2)}) copy-start(f32[512,512]{1,0:T(8,128)} %param.5) | copy-start | bytes 3145732
  28.2 21.6 %copy-start.8 = (f32[512,512]{1,0:T(8,128)S(1)}, f32[512,512]{1,0:T(8,128)}, u32[]{:S(2)}) copy-start(f32[512,512]{1,0:T(8,128)} %param.6) | copy-start | bytes 3145732
  28.4 21.5 %copy-start.3 = (f32[512,512]{1,0:T(8,128)S(1)}, f32[512,512]{1,0:T(8,128)}, u32[]{:S(2)}) copy-start(f32[512,512]{1,0:T(8,128)} %param.7) | copy-start | bytes 3145732
  28.4 2.7 collective-permute-start
  29.8 4.3 %collective-permute-start.1 = (f32[1,512]{1,0:T(1,128)S(1)}, f32[1,512]{1,0:T(1,128)S(1)}, u32[]{:S(2)}, u32[]{:S(2)}) collective-permute-start(f32[1,512]{1,0:T(1,128)S(1)} %get-tuple-element.27), channel_id=1, source_target_pairs={{8,0},{16,8},{24,16},{9,1},{17,9},{25,17},{10,2},{18,10},{26,18},{... | collective-permute-start | bytes 6152 | tf_op jit(solution)/shard_map/ppermute | solution.py:20
  34.3 9.4 %collective-permute-start.2 = (f32[514,1]{1,0:T(8,128)S(1)}, f32[514,1]{1,0:T(8,128)S(1)}, u32[]{:S(2)}, u32[]{:S(2)}) collective-permute-start(f32[514,1]{1,0:T(8,128)S(1)} %get-tuple-element.16), channel_id=1, source_target_pairs={{0,1},{1,2},{2,3},{3,4},{4,5},{5,6},{6,7},{8,9},{9,10},{10,11},{11... | collective-permute-start | bytes 6176 | tf_op jit(solution)/shard_map/ppermute | solution.py:18
  40.4 9.5 %collective-permute-start.3 = (f32[514,1]{1,0:T(8,128)S(1)}, f32[514,1]{1,0:T(8,128)S(1)}, u32[]{:S(2)}, u32[]{:S(2)}) collective-permute-start(f32[514,1]{1,0:T(8,128)S(1)} %get-tuple-element.17), channel_id=1, source_target_pairs={{1,0},{2,1},{3,2},{4,3},{5,4},{6,5},{7,6},{9,8},{10,9},{11,10},{12... | collective-permute-start | bytes 6176 | tf_op jit(solution)/shard_map/ppermute | solution.py:20
  50.7 1.0 copy-start.17
  73.2 27.7 %copy-start.9 = (f32[512,512]{1,0:T(8,128)S(1)}, f32[512,512]{1,0:T(8,128)}, u32[]{:S(2)}) copy-start(f32[512,512]{1,0:T(8,128)} %param.6) | copy-start | bytes 3145732
  75.4 25.5 %copy-start.4 = (f32[512,512]{1,0:T(8,128)S(1)}, f32[512,512]{1,0:T(8,128)}, u32[]{:S(2)}) copy-start(f32[512,512]{1,0:T(8,128)} %param.7) | copy-start | bytes 3145732
  75.4 4.9 %collective-permute-start.4 = (f32[1,512]{1,0:T(1,128)S(1)}, f32[1,512]{1,0:T(1,128)S(1)}, u32[]{:S(2)}, u32[]{:S(2)}) collective-permute-start(f32[1,512]{1,0:T(1,128)S(1)} %get-tuple-element.24), channel_id=1, source_target_pairs={{0,8},{8,16},{16,24},{1,9},{9,17},{17,25},{2,10},{10,18},{18,26},{... | collective-permute-start | bytes 6152 | tf_op jit(solution)/shard_map/ppermute | solution.py:18
  78.4 4.3 %collective-permute-start.5 = (f32[1,512]{1,0:T(1,128)S(1)}, f32[1,512]{1,0:T(1,128)S(1)}, u32[]{:S(2)}, u32[]{:S(2)}) collective-permute-start(f32[1,512]{1,0:T(1,128)S(1)} %get-tuple-element.25), channel_id=1, source_target_pairs={{8,0},{16,8},{24,16},{9,1},{17,9},{25,17},{10,2},{18,10},{26,18},{... | collective-permute-start | bytes 6152 | tf_op jit(solution)/shard_map/ppermute | solution.py:20
  82.9 11.0 %collective-permute-start.6 = (f32[514,1]{1,0:T(8,128)S(1)}, f32[514,1]{1,0:T(8,128)S(1)}, u32[]{:S(2)}, u32[]{:S(2)}) collective-permute-start(f32[514,1]{1,0:T(8,128)S(1)} %get-tuple-element.14), channel_id=1, source_target_pairs={{0,1},{1,2},{2,3},{3,4},{4,5},{5,6},{6,7},{8,9},{9,10},{10,11},{11... | collective-permute-start | bytes 6176 | tf_op jit(solution)/shard_map/ppermute | solution.py:18
  90.5 10.4 %collective-permute-start.7 = (f32[514,1]{1,0:T(8,128)S(1)}, f32[514,1]{1,0:T(8,128)S(1)}, u32[]{:S(2)}, u32[]{:S(2)}) collective-permute-start(f32[514,1]{1,0:T(8,128)S(1)} %get-tuple-element.15), channel_id=1, source_target_pairs={{1,0},{2,1},{3,2},{4,3},{5,4},{6,5},{7,6},{9,8},{10,9},{11,10},{12... | collective-permute-start | bytes 6176 | tf_op jit(solution)/shard_map/ppermute | solution.py:20
  101.8 1.0 copy-start.18
  126.9 29.0 %copy-start.10 = (f32[512,512]{1,0:T(8,128)S(1)}, f32[512,512]{1,0:T(8,128)}, u32[]{:S(2)}) copy-start(f32[512,512]{1,0:T(8,128)} %param.6) | copy-start | bytes 3145732
  129.9 26.9 %copy-start.2 = (f32[512,512]{1,0:T(8,128)}, f32[512,512]{1,0:T(8,128)S(1)}, u32[]{:S(2)}) copy-start(f32[512,512]{1,0:T(8,128)S(1)} %subtract_divide_fusion.1) | copy-start | bytes 3145732
  129.9 26.0 %copy-start.5 = (f32[512,512]{1,0:T(8,128)S(1)}, f32[512,512]{1,0:T(8,128)}, u32[]{:S(2)}) copy-start(f32[512,512]{1,0:T(8,128)} %param.7) | copy-start | bytes 3145732
  129.9 4.8 %collective-permute-start.8 = (f32[1,512]{1,0:T(1,128)S(1)}, f32[1,512]{1,0:T(1,128)S(1)}, u32[]{:S(2)}, u32[]{:S(2)}) collective-permute-start(f32[1,512]{1,0:T(1,128)S(1)} %get-tuple-element.22), channel_id=1, source_target_pairs={{0,8},{8,16},{16,24},{1,9},{9,17},{17,25},{2,10},{10,18},{18,26},{... | collective-permute-start | bytes 6152 | tf_op jit(solution)/shard_map/ppermute | solution.py:18
  133.4 4.3 %collective-permute-start.9 = (f32[1,512]{1,0:T(1,128)S(1)}, f32[1,512]{1,0:T(1,128)S(1)}, u32[]{:S(2)}, u32[]{:S(2)}) collective-permute-start(f32[1,512]{1,0:T(1,128)S(1)} %get-tuple-element.23), channel_id=1, source_target_pairs={{8,0},{16,8},{24,16},{9,1},{17,9},{25,17},{10,2},{18,10},{26,18},{... | collective-permute-start | bytes 6152 | tf_op jit(solution)/shard_map/ppermute | solution.py:20
  137.8 11.0 %collective-permute-start.10 = (f32[514,1]{1,0:T(8,128)S(1)}, f32[514,1]{1,0:T(8,128)S(1)}, u32[]{:S(2)}, u32[]{:S(2)}) collective-permute-start(f32[514,1]{1,0:T(8,128)S(1)} %get-tuple-element.12), channel_id=1, source_target_pairs={{0,1},{1,2},{2,3},{3,4},{4,5},{5,6},{6,7},{8,9},{9,10},{10,11},{11... | collective-permute-start | bytes 6176 | tf_op jit(solution)/shard_map/ppermute | solution.py:18
  145.5 10.4 %collective-permute-start.11 = (f32[514,1]{1,0:T(8,128)S(1)}, f32[514,1]{1,0:T(8,128)S(1)}, u32[]{:S(2)}, u32[]{:S(2)}) collective-permute-start(f32[514,1]{1,0:T(8,128)S(1)} %get-tuple-element.13), channel_id=1, source_target_pairs={{1,0},{2,1},{3,2},{4,3},{5,4},{6,5},{7,6},{9,8},{10,9},{11,10},{12... | collective-permute-start | bytes 6176 | tf_op jit(solution)/shard_map/ppermute | solution.py:20
  156.8 1.0 copy-start.16
  182.1 30.0 %copy-start.11 = (f32[512,512]{1,0:T(8,128)S(1)}, f32[512,512]{1,0:T(8,128)}, u32[]{:S(2)}) copy-start(f32[512,512]{1,0:T(8,128)} %param.6) | copy-start | bytes 3145732
  186.0 26.0 %copy-start.14 = (f32[512,512]{1,0:T(8,128)}, f32[512,512]{1,0:T(8,128)S(1)}, u32[]{:S(2)}) copy-start(f32[512,512]{1,0:T(8,128)S(1)} %subtract_divide_fusion) | copy-start | bytes 3145732
  186.1 26.0 %copy-start.6 = (f32[512,512]{1,0:T(8,128)S(1)}, f32[512,512]{1,0:T(8,128)}, u32[]{:S(2)}) copy-start(f32[512,512]{1,0:T(8,128)} %param.7) | copy-start | bytes 3145732
  186.1 4.8 %collective-permute-start.12 = (f32[1,512]{1,0:T(1,128)S(1)}, f32[1,512]{1,0:T(1,128)S(1)}, u32[]{:S(2)}, u32[]{:S(2)}) collective-permute-start(f32[1,512]{1,0:T(1,128)S(1)} %get-tuple-element.20), channel_id=1, source_target_pairs={{0,8},{8,16},{16,24},{1,9},{9,17},{17,25},{2,10},{10,18},{18,26},{... | collective-permute-start | bytes 6152 | tf_op jit(solution)/shard_map/ppermute | solution.py:18
  189.5 4.3 %collective-permute-start.13 = (f32[1,512]{1,0:T(1,128)S(1)}, f32[1,512]{1,0:T(1,128)S(1)}, u32[]{:S(2)}, u32[]{:S(2)}) collective-permute-start(f32[1,512]{1,0:T(1,128)S(1)} %get-tuple-element.21), channel_id=1, source_target_pairs={{8,0},{16,8},{24,16},{9,1},{17,9},{25,17},{10,2},{18,10},{26,18},{... | collective-permute-start | bytes 6152 | tf_op jit(solution)/shard_map/ppermute | solution.py:20
  194.0 11.0 %collective-permute-start.14 = (f32[514,1]{1,0:T(8,128)S(1)}, f32[514,1]{1,0:T(8,128)S(1)}, u32[]{:S(2)}, u32[]{:S(2)}) collective-permute-start(f32[514,1]{1,0:T(8,128)S(1)} %get-tuple-element.10), channel_id=1, source_target_pairs={{0,1},{1,2},{2,3},{3,4},{4,5},{5,6},{6,7},{8,9},{9,10},{10,11},{11... | collective-permute-start | bytes 6176 | tf_op jit(solution)/shard_map/ppermute | solution.py:18
  201.7 10.4 %collective-permute-start.15 = (f32[514,1]{1,0:T(8,128)S(1)}, f32[514,1]{1,0:T(8,128)S(1)}, u32[]{:S(2)}, u32[]{:S(2)}) collective-permute-start(f32[514,1]{1,0:T(8,128)S(1)} %get-tuple-element.11), channel_id=1, source_target_pairs={{1,0},{2,1},{3,2},{4,3},{5,4},{6,5},{7,6},{9,8},{10,9},{11,10},{12... | collective-permute-start | bytes 6176 | tf_op jit(solution)/shard_map/ppermute | solution.py:20
  255.1 28.2 %copy-start.12 = (f32[512,512]{1,0:T(8,128)S(1)}, f32[512,512]{1,0:T(8,128)}, u32[]{:S(2)}) copy-start(f32[512,512]{1,0:T(8,128)} %param.6) | copy-start | bytes 3145732
  257.2 27.9 %copy-start.15 = (f32[512,512]{1,0:T(8,128)}, f32[512,512]{1,0:T(8,128)S(1)}, u32[]{:S(2)}) copy-start(f32[512,512]{1,0:T(8,128)S(1)} %multiply_add_fusion) | copy-start | bytes 3145732
  257.2 26.0 %copy-start.7 = (f32[512,512]{1,0:T(8,128)S(1)}, f32[512,512]{1,0:T(8,128)}, u32[]{:S(2)}) copy-start(f32[512,512]{1,0:T(8,128)} %param.7) | copy-start | bytes 3145732
  257.3 4.8 %collective-permute-start.16 = (f32[1,512]{1,0:T(1,128)S(1)}, f32[1,512]{1,0:T(1,128)S(1)}, u32[]{:S(2)}, u32[]{:S(2)}) collective-permute-start(f32[1,512]{1,0:T(1,128)S(1)} %get-tuple-element.18), channel_id=1, source_target_pairs={{0,8},{8,16},{16,24},{1,9},{9,17},{17,25},{2,10},{10,18},{18,26},{... | collective-permute-start | bytes 6152 | tf_op jit(solution)/shard_map/ppermute | solution.py:18
  260.7 4.3 %collective-permute-start.17 = (f32[1,512]{1,0:T(1,128)S(1)}, f32[1,512]{1,0:T(1,128)S(1)}, u32[]{:S(2)}, u32[]{:S(2)}) collective-permute-start(f32[1,512]{1,0:T(1,128)S(1)} %get-tuple-element.19), channel_id=1, source_target_pairs={{8,0},{16,8},{24,16},{9,1},{17,9},{25,17},{10,2},{18,10},{26,18},{... | collective-permute-start | bytes 6152 | tf_op jit(solution)/shard_map/ppermute | solution.py:20
  265.2 11.0 %collective-permute-start.18 = (f32[514,1]{1,0:T(8,128)S(1)}, f32[514,1]{1,0:T(8,128)S(1)}, u32[]{:S(2)}, u32[]{:S(2)}) collective-permute-start(f32[514,1]{1,0:T(8,128)S(1)} %get-tuple-element.8), channel_id=1, source_target_pairs={{0,1},{1,2},{2,3},{3,4},{4,5},{5,6},{6,7},{8,9},{9,10},{10,11},{11... | collective-permute-start | bytes 6176 | tf_op jit(solution)/shard_map/ppermute | solution.py:18
  272.9 10.4 %collective-permute-start.19 = (f32[514,1]{1,0:T(8,128)S(1)}, f32[514,1]{1,0:T(8,128)S(1)}, u32[]{:S(2)}, u32[]{:S(2)}) collective-permute-start(f32[514,1]{1,0:T(8,128)S(1)} %get-tuple-element.9), channel_id=1, source_target_pairs={{1,0},{2,1},{3,2},{4,3},{5,4},{6,5},{7,6},{9,8},{10,9},{11,10},{12... | collective-permute-start | bytes 6176 | tf_op jit(solution)/shard_map/ppermute | solution.py:20
